TPU v7x, 128 devices: a whole 4x4x4 slice. The times are simulated.
128 devices in a mesh: space: 16 (over z_hi, x, core), chan: 8 (over y, z_lo).
Axes of the slice: x: 4, y: 4, z: 4 (z_hi: 2, z_lo: 2; z = z_hi * 2 + z_lo), core: 2. Of those that a mesh axis runs over, the one named last changes fastest.
Arguments:
- inputs: bfloat16 [128, 64, 32, 128], P('chan', 'space'), may hold values from -6 to 6
- filters: bfloat16 [27, 128, 128], P(None, 'chan'), may hold values from -0.109375 to 0.109375
- cotangent: bfloat16 [128, 64, 32, 128], P('chan', 'space'), may hold values from -6 to 6
Outputs:
- grad_inputs: bfloat16 [128, 64, 32, 128], P('chan', 'space')
- grad_filters: float32 [27, 128, 128], P(None, 'chan')
All inputs are finite; a program needn't handle non-finite values.
Results may differ from a plain program's by a relative error of at most 0.0049.
Values may be sent and summed in bfloat16 or wider, within the bound.
A program may use at most 128 MiB of HBM per device.

v0:
```python
import math
import jax
import jax.numpy as jnp
from jax import lax
from jax.sharding import PartitionSpec as P


def with_halo(block, sides, width):
    for axis, dim in sides:
        count = lax.axis_size(axis)
        forward = [(i, i + 1) for i in range(count - 1)]
        backward = [(target, source) for source, target in forward]
        low = lax.ppermute(
            lax.slice_in_dim(block, block.shape[dim] - width, None, axis=dim), axis, forward
        )
        high = lax.ppermute(lax.slice_in_dim(block, 0, width, axis=dim), axis, backward)
        block = jnp.concatenate([low, block, high], axis=dim)
    return block


def shifted(padded, depth_off, row_off, column_off, plane_count, row_count, column_count):
    return padded[
        :,
        depth_off : depth_off + plane_count,
        row_off : row_off + row_count,
        column_off : column_off + column_count,
    ]


def forward_part(padded, weights, plane_count, row_count, column_count):
    total = None
    for depth_off in range(3):
        stacked = jnp.concatenate(
            [
                shifted(
                    padded, depth_off, inner // 3, inner % 3, plane_count, row_count, column_count
                )
                for inner in range(9)
            ],
            axis=0,
        )
        block = weights[9 * depth_off : 9 * depth_off + 9].reshape(
            9 * weights.shape[1], weights.shape[2]
        )
        term = jnp.einsum("io,idhw->odhw", block, stacked, preferred_element_type=jnp.float32)
        total = term if total is None else total + term
    return total


def body(inputs, filters, cotangent):
    plane_count = inputs.shape[1]
    row_count = inputs.shape[2]
    column_count = inputs.shape[3]
    in_rim = with_halo(inputs, (("space", 1),), 1)
    in_pad = jnp.pad(in_rim, ((0, 0), (0, 0), (1, 1), (1, 1)))
    partial_sum = forward_part(in_pad, filters, plane_count, row_count, column_count)
    pre_act = lax.psum_scatter(partial_sum, "chan", scatter_dimension=0, tiled=True)
    sigma = jax.nn.sigmoid(pre_act)
    grad_out = (cotangent.astype(jnp.float32) * sigma * (1.0 + pre_act * (1.0 - sigma))).astype(
        jnp.bfloat16
    )
    grad_all = lax.all_gather(grad_out, "chan", axis=0, tiled=True)
    grad_rim = with_halo(grad_all, (("space", 1),), 1)
    grad_pad = jnp.pad(grad_rim, ((0, 0), (0, 0), (1, 1), (1, 1)))
    grad_in = None
    for offset in range(27):
        depth_off = offset // 9
        row_off = offset // 3 % 3
        column_off = offset % 3
        window = shifted(
            grad_pad,
            2 - depth_off,
            2 - row_off,
            2 - column_off,
            plane_count,
            row_count,
            column_count,
        )
        term = jnp.einsum(
            "io,odhw->idhw", filters[offset], window, preferred_element_type=jnp.float32
        )
        grad_in = term if grad_in is None else grad_in + term
    stacked_in = jnp.stack(
        [
            shifted(
                in_pad,
                offset // 9,
                offset // 3 % 3,
                offset % 3,
                plane_count,
                row_count,
                column_count,
            )
            for offset in range(27)
        ]
    )
    grad_w = jnp.einsum("kidhw,odhw->kio", stacked_in, grad_all, preferred_element_type=jnp.float32)
    grad_w = lax.psum(grad_w, "space")
    cell_total = plane_count * lax.axis_size("space") * row_count * column_count
    return (grad_in.astype(jnp.bfloat16), grad_w * (1.0 / math.sqrt(cell_total)))


def solution(mesh):
    placed = (P("chan", "space", None, None), P(None, "chan", None), P("chan", "space", None, None))
    return jax.shard_map(
        body,
        mesh=mesh,
        in_specs=placed,
        out_specs=(P("chan", "space", None, None), P(None, "chan", None)),
        check_vma=False,
    )
```

profile of v0, /device:TPU:7, one launch (start us, length us, event | category | flops | bytes accessed | tf_op | source)
XLA Modules:
  0.0 548.7 jit_solution(15890602798667119826)
XLA Ops:
  8.6 6.0 %collective-permute-start = (bf16[16,1,32,128]{3,0,2,1:T(8,128)(2,1)S(1)}, bf16[16,1,32,128]{3,0,2,1:T(8,128)(2,1)S(1)}, u32[]{:S(2)}, u32[]{:S(2)}) collective-permute-start(bf16[16,1,32,128]{3,0,2,1:T(8,128)(2,1)S(1)} %get-tuple-element.34), channel_id=1, source_target_pairs={{0,8},{8,16},{16,24},{24,32},{32,40},{40,48},{48,56},{56,64},{64,7... | collective-permute-start | bytes 393224 | tf_op jit(solution)/shard_map/ppermute | solution.py:13
  14.6 1.9 collective-permute-start.1
  17.4 7.1 %collective-permute-done.1 = bf16[16,1,32,128]{3,0,2,1:T(8,128)(2,1)S(1)} collective-permute-done((bf16[16,1,32,128]{3,0,2,1:T(8,128)(2,1)S(1)}, bf16[16,1,32,128]{3,0,2,1:T(8,128)(2,1)S(1)}, u32[]{:S(2)}, u32[]{:S(2)}) %collective-permute-start.1) | collective-permute-done | bytes 131104 | tf_op jit(solution)/shard_map/ppermute | solution.py:16
  31.5 2.5 fusion.245
  34.0 2.5 fusion.246
  36.4 5.7 %add_bitcast_fusion = f32[128,4,32,128]{0,3,2,1:T(8,128)} fusion(f32[4,32,128,128]{3,2,1,0:T(8,128)S(1)} %fusion.245, f32[4,32,128,128]{3,2,1,0:T(8,128)S(1)} %fusion.246, bf16[144,4,32,128]{3,0,2,1:T(8,128)(2,1)S(1)} %get-tuple-element.8, bf16[144,128,1,1]{1,0,3,2:T(8,128)(2,1)S(1)} %bitcast.324), kind=kOutput, calls=%fused_computation.12 | convolution fusion | flops 608174080 | bytes 29921280 | tf_op jit(solution)/shard_map/io,idhw->odhw/dot_general | solution.py:45
  42.1 10.7 %copy.48 = f32[128,4,32,128]{3,2,1,0:T(8,128)} copy(f32[128,4,32,128]{0,3,2,1:T(8,128)} %add_bitcast_fusion) | data formatting | bytes 16777216 | tf_op jit(solution)/shard_map/add | solution.py:46
  52.9 167.8 %reduce-scatter.2.cloned.1.call-done = f32[16,4,32,128]{3,2,1,0:T(8,128)} async-done(((f32[128,4,32,128]{3,2,1,0:T(8,128)}), f32[16,4,32,128]{3,2,1,0:T(8,128)}) %reduce-scatter.2.cloned.1.call-update) | async-done | bytes 1048592 | tf_op jit(solution)/shard_map/reduce_scatter | solution.py:57
  220.7 2.4 multiply_convert_fusion
  249.5 63.8 %all-gather.2.cloned.1.call-done = bf16[128,4,32,128]{3,2,1,0:T(8,128)(2,1)} async-done(((bf16[16,4,32,128]{3,2,1,0:T(8,128)(2,1)}), bf16[128,4,32,128]{3,2,1,0:T(8,128)(2,1)}) %all-gather.2.cloned.1.call-update) | async-done | bytes 4194320 | tf_op jit(solution)/shard_map/all_gather | solution.py:62
  313.3 5.0 copy.49
  318.4 2.0 copy-done
  321.6 3.3 collective-permute-start.3
  324.8 5.9 %collective-permute-start.2 = (bf16[128,1,32,128]{3,0,2,1:T(8,128)(2,1)S(1)}, bf16[128,1,32,128]{3,0,2,1:T(8,128)(2,1)S(1)}, u32[]{:S(2)}, u32[]{:S(2)}) collective-permute-start(bf16[128,1,32,128]{3,0,2,1:T(8,128)(2,1)S(1)} %get-tuple-element.6), channel_id=1, source_target_pairs={{0,8},{8,16},{16,24},{24,32},{32,40},{40,48},{48,56},{56,64},{64,7... | collective-permute-start | bytes 3145736 | tf_op jit(solution)/shard_map/ppermute | solution.py:13
  330.8 7.9 %fusion.179 = f32[27,16,128]{2,1,0:T(8,128)} fusion(bf16[27,16,4,32,128]{4,1,3,2,0:T(8,128)(2,1)} %bitcast_dynamic-update-slice_fusion, bf16[128,4,32,128,1]{3,2,1,0,4:T(8,128)(2,1)S(1)} %bitcast.323), kind=kOutput, calls=%fused_computation.120 | convolution fusion | flops 1811939328 | bytes 18571264 | tf_op jit(solution)/shard_map/kidhw,odhw->kio/dot_general | solution.py:97
  338.6 5.5 %fusion.197 = f32[4,32,128,16]{2,3,1,0:T(8,128)} fusion(bf16[27,16,128]{2,1,0:T(8,128)(2,1)S(1)} %copy-done.11, bf16[128,4,32,128]{3,2,1,0:T(8,128)(2,1)} %all-gather.2.cloned.1.call-done), kind=kOutput, calls=%fused_computation.192 | convolution fusion | flops 67108864 | bytes 5246976 | tf_op jit(solution)/shard_map/io,odhw->idhw/dot_general | solution.py:79
  344.1 131.4 %all-reduce.4.cloned.1.call-done = f32[27,16,128]{2,1,0:T(8,128)} async-done(((f32[27,16,128]{2,1,0:T(8,128)}), f32[27,16,128]{2,1,0:T(8,128)}) %all-reduce.4.cloned.1.call-update) | async-done | bytes 221200 | tf_op jit(solution)/shard_map/psum | solution.py:98
  477.1 9.9 %select_maximum_fusion = bf16[128,6,34,130]{3,0,2,1:T(8,128)(2,1)S(1)} fusion(bf16[128,1,32,128]{3,0,2,1:T(8,128)(2,1)S(1)} %collective-permute-done.3, bf16[128,4,32,128]{3,0,2,1:T(8,128)(2,1)} %copy-done, bf16[128,1,32,128]{3,0,2,1:T(8,128)(2,1)S(1)} %collective-permute-done.2), kind=kLoop, calls=%fused_computation.7 | loop fusion | flops 64496640 | bytes 13080576 | tf_op jit(solution)/shard_map/concatenate | solution.py:17
  490.2 2.6 fusion.36
  492.7 2.5 fusion.38
  495.3 1.7 fusion.40
  497.0 2.5 fusion.42
  499.5 2.5 fusion.44
  502.0 1.7 fusion.46
  503.6 2.5 fusion.50
  506.1 1.7 fusion.52
  507.8 2.7 fusion.54
  517.9 2.5 fusion.85
  520.4 1.7 fusion.89
  522.1 2.5 fusion.92
  524.6 2.8 fusion.95
  530.6 6.3 %fusion.173 = f32[4,32,128,16]{2,3,1,0:T(8,128)S(1)} fusion(f32[4,32,128,16]{2,3,1,0:T(8,128)S(1)} %copy-done.4, f32[4,32,128,16]{2,3,1,0:T(8,128)S(1)} %fusion.32, f32[4,32,128,16]{2,3,1,0:T(8,128)} %fusion.34, f32[4,32,128,16]{2,3,1,0:T(8,128)} %fusion.36, f32[4,32,128,16]{2,3,1,0:T(8,128)} %fusion.38, f32[4,32,128,16]{2,3,1,0:T(8,128)} %fusion.40, ...), kind=kOutput, calls=%fused_computation.118 | convolution fusion | flops 70516736 | bytes 18878464 | tf_op jit(solution)/shard_map/io,odhw->idhw/dot_general | solution.py:79
  (87 shorter events, 57.0 us)
Async XLA Ops:
  7.2 213.5 %reduce-scatter.2.cloned.1.call-start = ((), (), s32[]{:S(2)}) async-start(), calls=%async_computation.1 | async-start | bytes 9437184 | tf_op jit(solution)/shard_map/reduce_scatter | solution.py:57
  8.6 8.7 %collective-permute-start = (bf16[16,1,32,128]{3,0,2,1:T(8,128)(2,1)S(1)}, bf16[16,1,32,128]{3,0,2,1:T(8,128)(2,1)S(1)}, u32[]{:S(2)}, u32[]{:S(2)}) collective-permute-start(bf16[16,1,32,128]{3,0,2,1:T(8,128)(2,1)S(1)} %get-tuple-element.34), channel_id=1, source_target_pairs={{0,8},{8,16},{16,24},{24,32},{32,40},{40,48},{48,56},{56,64},{64,7... | collective-permute-start | bytes 393224 | tf_op jit(solution)/shard_map/ppermute | solution.py:13
  14.6 9.9 %collective-permute-start.1 = (bf16[16,1,32,128]{3,0,2,1:T(8,128)(2,1)S(1)}, bf16[16,1,32,128]{3,0,2,1:T(8,128)(2,1)S(1)}, u32[]{:S(2)}, u32[]{:S(2)}) collective-permute-start(bf16[16,1,32,128]{3,0,2,1:T(8,128)(2,1)S(1)} %get-tuple-element.35), channel_id=1, source_target_pairs={{8,0},{16,8},{24,16},{32,24},{40,32},{48,40},{56,48},{64,56},{72,6... | collective-permute-start | bytes 393224 | tf_op jit(solution)/shard_map/ppermute | solution.py:16
  25.8 2.0 copy-start.3
  52.8 167.9 %copy-start.10 = (bf16[16,4,32,128]{3,2,1,0:T(8,128)(2,1)S(1)}, bf16[16,4,32,128]{3,2,1,0:T(8,128)(2,1)}, u32[]{:S(2)}) copy-start(bf16[16,4,32,128]{3,2,1,0:T(8,128)(2,1)} %param.5) | copy-start | bytes 1572868
  52.8 260.5 %all-gather.2.cloned.1.call-start = ((), (), s32[]{:S(2)}) async-start(), calls=%async_computation.2 | async-start | bytes 4718592 | tf_op jit(solution)/shard_map/all_gather | solution.py:62
  223.1 252.4 %all-reduce.4.cloned.1.call-start = ((), (), s32[]{:S(2)}) async-start(), calls=%async_computation.3 | async-start | bytes 442368 | tf_op jit(solution)/shard_map/psum | solution.py:98
  313.3 17.4 %copy-start.2 = (bf16[128,4,32,128]{3,2,1,0:T(8,128)(2,1)S(1)}, bf16[128,4,32,128]{3,2,1,0:T(8,128)(2,1)}, u32[]{:S(2)}) copy-start(bf16[128,4,32,128]{3,2,1,0:T(8,128)(2,1)} %all-gather.2.cloned.1.call-done) | copy-start | bytes 12582916
  318.4 2.0 copy-start
  321.6 155.6 %collective-permute-start.3 = (bf16[128,1,32,128]{3,0,2,1:T(8,128)(2,1)}, bf16[128,1,32,128]{3,0,2,1:T(8,128)(2,1)S(1)}, u32[]{:S(2)}, u32[]{:S(2)}) collective-permute-start(bf16[128,1,32,128]{3,0,2,1:T(8,128)(2,1)} %get-tuple-element.7), channel_id=1, source_target_pairs={{8,0},{16,8},{24,16},{32,24},{40,32},{48,40},{56,48},{64,56},{72,6... | collective-permute-start | bytes 3145736 | tf_op jit(solution)/shard_map/ppermute | solution.py:16
  324.8 152.3 %collective-permute-start.2 = (bf16[128,1,32,128]{3,0,2,1:T(8,128)(2,1)S(1)}, bf16[128,1,32,128]{3,0,2,1:T(8,128)(2,1)S(1)}, u32[]{:S(2)}, u32[]{:S(2)}) collective-permute-start(bf16[128,1,32,128]{3,0,2,1:T(8,128)(2,1)S(1)} %get-tuple-element.6), channel_id=1, source_target_pairs={{0,8},{8,16},{16,24},{24,32},{32,40},{40,48},{48,56},{56,64},{64,7... | collective-permute-start | bytes 3145736 | tf_op jit(solution)/shard_map/ppermute | solution.py:13
  330.7 7.9 %copy-start.11 = (bf16[27,16,128]{2,1,0:T(8,128)(2,1)S(1)}, bf16[27,16,128]{2,1,0:T(8,128)(2,1)}, u32[]{:S(2)}) copy-start(bf16[27,16,128]{2,1,0:T(8,128)(2,1)} %param.4) | copy-start | bytes 331780
  524.6 4.4 copy-start.1
  527.3 3.3 copy-start.4
  536.9 1.2 copy-start.5
  536.9 1.5 copy-start.6
  536.9 1.8 copy-start.7
  536.9 2.1 copy-start.8
  537.0 2.5 copy-start.9
Sparse Core Ops, SparseCore 0:
  52.9 167.6 reduce-scatter.1
  223.3 90.0 all-gather.1
  338.8 136.7 all-reduce.3
where the time goes:
time: 558 us; the launch traced here: 549 us
  waiting for transfers between devices  370 us (66%)
  matrix products  75.9 us (14%)
  local copies, waits for them, and re-layouts  53.7 us (10%)
  other arithmetic  17.3 us (3%)
  starting transfers between devices  17.2 us (3%)
  between operations  14.5 us (3%)
    reduce_scatter x1, waiting for transfers between devices, body(): lax.psum_scatter(partial_sum, 'chan', scatter_dimension=0, tiled=True)  168 us
    psum x1, waiting for transfers between devices, body(): grad_w = lax.psum(grad_w, 'space')  131 us
    all_gather x1, waiting for transfers between devices, body(): grad_all = lax.all_gather(grad_out, 'chan', axis=0, tiled=True)  63.8 us
    dot_general x27, matrix products, body(): jnp.einsum('io,odhw->idhw', filters[offset], window, preferred_element_ty...  57.4 us
    unnamed x57, local copies, waits for them, and re-layouts  34.1 us
    ppermute x2, starting transfers between devices, with_halo(): lax.ppermute(lax.slice_in_dim(block, block.shape[dim] - width, None, axis...  11.9 us
  transfers between devices with their start and end apart: 7, of which 4 were waited for; matrix products, arithmetic and copies ran while one was open for 8% of the time, Pallas kernels for 0%

commit v1 on v0

--- a/solution.py
+++ b/solution.py
@@ -59,7 +59,12 @@
     grad_out = (cotangent.astype(jnp.float32) * sigma * (1.0 + pre_act * (1.0 - sigma))).astype(
         jnp.bfloat16
     )
-    grad_all = lax.all_gather(grad_out, "chan", axis=0, tiled=True)
+    grad_all = jnp.concatenate(
+        jax.lax.all_to_all(
+            jnp.stack(tuple((grad_out for _ in range(jax.lax.axis_size("chan"))))), "chan", 0, 0
+        ),
+        0,
+    )
     grad_rim = with_halo(grad_all, (("space", 1),), 1)
     grad_pad = jnp.pad(grad_rim, ((0, 0), (0, 0), (1, 1), (1, 1)))
     grad_in = None

time: 558 us -> 528 us (0.946)
  waiting for transfers between devices: 370 us -> 338 us
    all_gather x1 -> x0, waiting for transfers between devices: 63.8 us -> none  [body(): grad_all = lax.all_gather(grad_out, 'chan', axis=0, tiled=True)]
    all_to_all x0 -> x1, waiting for transfers between devices: none -> 43.2 us  [body(): jax.lax.all_to_all(jnp.stack(tuple((grad_out for _ in range(jax.lax.axis_...]
    reduce_scatter x1, waiting for transfers between devices: 168 us -> 157 us  [body(): lax.psum_scatter(partial_sum, 'chan', scatter_dimension=0, tiled=True)]
    unnamed x57 -> x55, local copies, waits for them, and re-layouts: 34.1 us -> 32 us
where the time goes in v1:
time: 528 us; the launch traced here: 518 us
  waiting for transfers between devices  338 us (64%)
  matrix products  74.2 us (14%)
  local copies, waits for them, and re-layouts  53.4 us (10%)
  starting transfers between devices  21.7 us (4%)
  other arithmetic  16.5 us (3%)
  between operations  14.5 us (3%)
    reduce_scatter x1, waiting for transfers between devices, body(): lax.psum_scatter(partial_sum, 'chan', scatter_dimension=0, tiled=True)  157 us
    psum x1, waiting for transfers between devices, body(): grad_w = lax.psum(grad_w, 'space')  130 us
    dot_general x27, matrix products, body(): jnp.einsum('io,odhw->idhw', filters[offset], window, preferred_element_ty...  55.8 us
    all_to_all x1, waiting for transfers between devices, body(): jax.lax.all_to_all(jnp.stack(tuple((grad_out for _ in range(jax.lax.axis_...  43.2 us
    unnamed x55, local copies, waits for them, and re-layouts  32 us
    ppermute x2, starting transfers between devices, with_halo(): lax.ppermute(lax.slice_in_dim(block, block.shape[dim] - width, None, axis...  11.8 us
    concatenate x2, other arithmetic, with_halo(): block = jnp.concatenate([low, block, high], axis=dim)  11 us
    dot_general x3, matrix products, forward_part(): jnp.einsum('io,idhw->odhw', block, stacked, preferred_element_type=jnp.fl...  10.6 us
  transfers between devices with their start and end apart: 7, of which 4 were waited for; matrix products, arithmetic and copies ran while one was open for 8% of the time, Pallas kernels for 0%

profile of v1, /device:TPU:7, one launch (start us, length us, event | category | flops | bytes accessed | tf_op | source)
XLA Modules:
  0.0 518.0 jit_solution(7903634146987105464)
XLA Ops:
  8.6 6.0 %collective-permute-start = (bf16[16,1,32,128]{3,0,2,1:T(8,128)(2,1)S(1)}, bf16[16,1,32,128]{3,0,2,1:T(8,128)(2,1)S(1)}, u32[]{:S(2)}, u32[]{:S(2)}) collective-permute-start(bf16[16,1,32,128]{3,0,2,1:T(8,128)(2,1)S(1)} %get-tuple-element.34), channel_id=1, source_target_pairs={{0,8},{8,16},{16,24},{24,32},{32,40},{40,48},{48,56},{56,64},{64,7... | collective-permute-start | bytes 393224 | tf_op jit(solution)/shard_map/ppermute | solution.py:13
  14.6 1.9 collective-permute-start.1
  17.4 7.1 %collective-permute-done.1 = bf16[16,1,32,128]{3,0,2,1:T(8,128)(2,1)S(1)} collective-permute-done((bf16[16,1,32,128]{3,0,2,1:T(8,128)(2,1)S(1)}, bf16[16,1,32,128]{3,0,2,1:T(8,128)(2,1)S(1)}, u32[]{:S(2)}, u32[]{:S(2)}) %collective-permute-start.1) | collective-permute-done | bytes 131104 | tf_op jit(solution)/shard_map/ppermute | solution.py:16
  31.5 2.5 fusion.238
  34.0 2.5 fusion.239
  36.4 5.7 %add_bitcast_fusion = f32[128,4,32,128]{0,3,2,1:T(8,128)} fusion(f32[4,32,128,128]{3,2,1,0:T(8,128)S(1)} %fusion.238, f32[4,32,128,128]{3,2,1,0:T(8,128)S(1)} %fusion.239, bf16[144,4,32,128]{3,0,2,1:T(8,128)(2,1)S(1)} %get-tuple-element.8, bf16[144,128,1,1]{1,0,3,2:T(8,128)(2,1)S(1)} %bitcast.332), kind=kOutput, calls=%fused_computation.12 | convolution fusion | flops 608174080 | bytes 29921280 | tf_op jit(solution)/shard_map/io,idhw->odhw/dot_general | solution.py:45
  42.2 10.5 %copy.21 = f32[128,4,32,128]{3,2,1,0:T(8,128)} copy(f32[128,4,32,128]{0,3,2,1:T(8,128)} %add_bitcast_fusion) | data formatting | bytes 16777216 | tf_op jit(solution)/shard_map/add | solution.py:46
  63.2 157.3 %reduce-scatter.2.cloned.1.call-done = f32[16,4,32,128]{3,2,1,0:T(8,128)} async-done(((f32[128,4,32,128]{3,2,1,0:T(8,128)}), f32[16,4,32,128]{3,2,1,0:T(8,128)}) %reduce-scatter.2.cloned.1.call-update) | async-done | bytes 1048592 | tf_op jit(solution)/shard_map/reduce_scatter | solution.py:57
  220.6 1.6 multiply_convert_fusion
  222.6 3.0 stack.95
  225.6 4.6 all-to-all-start
  246.0 43.2 %all-to-all-done = bf16[8,16,4,32,128]{4,1,3,2,0:T(8,128)(2,1)} async-done(((bf16[8,16,4,32,128]{4,1,3,2,0:T(8,128)(2,1)}), bf16[8,16,4,32,128]{4,1,3,2,0:T(8,128)(2,1)}, u32[]{:S(2)}, u32[]{:S(2)}) %all-to-all-start) | async-done | bytes 4194336 | tf_op jit(solution)/shard_map/all_to_all | solution.py:63
  289.2 3.4 copy.23
  293.9 3.4 collective-permute-start.3
  297.3 5.8 %collective-permute-start.2 = (bf16[128,1,32,128]{3,0,2,1:T(8,128)(2,1)S(1)}, bf16[128,1,32,128]{3,0,2,1:T(8,128)(2,1)S(1)}, u32[]{:S(2)}, u32[]{:S(2)}) collective-permute-start(bf16[128,1,32,128]{3,0,2,1:T(8,128)(2,1)S(1)} %get-tuple-element.6), channel_id=1, source_target_pairs={{0,8},{8,16},{16,24},{24,32},{32,40},{40,48},{48,56},{56,64},{64,7... | collective-permute-start | bytes 3145736 | tf_op jit(solution)/shard_map/ppermute | solution.py:13
  303.1 7.7 %convolution_bitcast_fusion = f32[27,16,128]{2,1,0:T(8,128)} fusion(bf16[27,16,4,32,128]{4,1,3,2,0:T(8,128)(2,1)} %bitcast_dynamic-update-slice_fusion, bf16[128,4,32,128,1]{3,0,2,1,4:T(8,128)(2,1)S(1)} %bitcast.327), kind=kOutput, calls=%fused_computation.117 | convolution fusion | flops 1811939328 | bytes 18571264 | tf_op jit(solution)/shard_map/kidhw,odhw->kio/dot_general | solution.py:102
  310.9 3.8 fusion.191
  314.7 129.9 %all-reduce.4.cloned.1.call-done = f32[27,16,128]{2,1,0:T(8,128)} async-done(((f32[27,16,128]{2,1,0:T(8,128)}), f32[27,16,128]{2,1,0:T(8,128)}) %all-reduce.4.cloned.1.call-update) | async-done | bytes 221200 | tf_op jit(solution)/shard_map/psum | solution.py:103
  446.3 9.9 %select_maximum_fusion = bf16[128,6,34,130]{3,0,2,1:T(8,128)(2,1)S(1)} fusion(bf16[128,1,32,128]{3,0,2,1:T(8,128)(2,1)S(1)} %collective-permute-done.3, bf16[128,4,32,128]{3,0,2,1:T(8,128)(2,1)} %bitcast.329, bf16[128,1,32,128]{3,0,2,1:T(8,128)(2,1)S(1)} %collective-permute-done.2), kind=kLoop, calls=%fused_computation.7 | loop fusion | flops 64496640 | bytes 13080576 | tf_op jit(solution)/shard_map/concatenate | solution.py:17
  459.3 2.6 fusion.36
  461.9 2.6 fusion.38
  464.5 1.7 fusion.40
  466.2 2.5 fusion.42
  468.7 2.5 fusion.44
  471.2 1.7 fusion.46
  472.8 2.5 fusion.50
  477.0 2.9 fusion.54
  487.3 2.5 fusion.82
  489.8 1.7 fusion.86
  491.5 2.5 fusion.89
  493.9 2.7 fusion.92
  499.9 6.3 %fusion.170 = f32[4,32,128,16]{2,3,1,0:T(8,128)S(1)} fusion(f32[4,32,128,16]{2,3,1,0:T(8,128)S(1)} %copy-done.3, f32[4,32,128,16]{2,3,1,0:T(8,128)S(1)} %fusion.32, f32[4,32,128,16]{2,3,1,0:T(8,128)} %fusion.34, f32[4,32,128,16]{2,3,1,0:T(8,128)} %fusion.36, f32[4,32,128,16]{2,3,1,0:T(8,128)} %fusion.38, f32[4,32,128,16]{2,3,1,0:T(8,128)} %fusion.40, ...), kind=kOutput, calls=%fused_computation.115 | convolution fusion | flops 70516736 | bytes 18878464 | tf_op jit(solution)/shard_map/io,odhw->idhw/dot_general | solution.py:84
  (86 shorter events, 59.1 us)
Async XLA Ops:
  7.2 213.4 %reduce-scatter.2.cloned.1.call-start = ((), (), s32[]{:S(2)}) async-start(), calls=%async_computation.2 | async-start | bytes 9437184 | tf_op jit(solution)/shard_map/reduce_scatter | solution.py:57
  8.6 8.7 %collective-permute-start = (bf16[16,1,32,128]{3,0,2,1:T(8,128)(2,1)S(1)}, bf16[16,1,32,128]{3,0,2,1:T(8,128)(2,1)S(1)}, u32[]{:S(2)}, u32[]{:S(2)}) collective-permute-start(bf16[16,1,32,128]{3,0,2,1:T(8,128)(2,1)S(1)} %get-tuple-element.34), channel_id=1, source_target_pairs={{0,8},{8,16},{16,24},{24,32},{32,40},{40,48},{48,56},{56,64},{64,7... | collective-permute-start | bytes 393224 | tf_op jit(solution)/shard_map/ppermute | solution.py:13
  14.6 9.9 %collective-permute-start.1 = (bf16[16,1,32,128]{3,0,2,1:T(8,128)(2,1)S(1)}, bf16[16,1,32,128]{3,0,2,1:T(8,128)(2,1)S(1)}, u32[]{:S(2)}, u32[]{:S(2)}) collective-permute-start(bf16[16,1,32,128]{3,0,2,1:T(8,128)(2,1)S(1)} %get-tuple-element.35), channel_id=1, source_target_pairs={{8,0},{16,8},{24,16},{32,24},{40,32},{48,40},{56,48},{64,56},{72,6... | collective-permute-start | bytes 393224 | tf_op jit(solution)/shard_map/ppermute | solution.py:16
  25.8 2.0 copy-start.2
  54.6 165.9 %copy-start.9 = (bf16[16,4,32,128]{3,2,1,0:T(8,128)(2,1)S(1)}, bf16[16,4,32,128]{3,2,1,0:T(8,128)(2,1)}, u32[]{:S(2)}) copy-start(bf16[16,4,32,128]{3,2,1,0:T(8,128)(2,1)} %param.5) | copy-start | bytes 1572868
  225.6 63.6 %all-to-all-start = ((bf16[8,16,4,32,128]{4,1,3,2,0:T(8,128)(2,1)}), bf16[8,16,4,32,128]{4,1,3,2,0:T(8,128)(2,1)}, u32[]{:S(2)}, u32[]{:S(2)}) async-start(bf16[8,16,4,32,128]{4,1,3,2,0:T(8,128)(2,1)} %stack.95), calls=%async_computation.1 | async-start | bytes 8388608 | tf_op jit(solution)/shard_map/all_to_all | solution.py:63
  230.1 214.5 %all-reduce.4.cloned.1.call-start = ((), (), s32[]{:S(2)}) async-start(), calls=%async_computation.3 | async-start | bytes 442368 | tf_op jit(solution)/shard_map/psum | solution.py:103
  292.6 10.5 %copy-start = (bf16[8,16,4,32,128]{4,1,0,3,2:T(8,128)(2,1)}, bf16[8,16,4,32,128]{4,1,0,3,2:T(8,128)(2,1)S(1)}, u32[]{:S(2)}) copy-start(bf16[8,16,4,32,128]{4,1,0,3,2:T(8,128)(2,1)S(1)} %copy.23) | copy-start | bytes 12582916
  293.9 152.4 %collective-permute-start.3 = (bf16[128,1,32,128]{3,0,2,1:T(8,128)(2,1)}, bf16[128,1,32,128]{3,0,2,1:T(8,128)(2,1)S(1)}, u32[]{:S(2)}, u32[]{:S(2)}) collective-permute-start(bf16[128,1,32,128]{3,0,2,1:T(8,128)(2,1)} %get-tuple-element.7), channel_id=1, source_target_pairs={{8,0},{16,8},{24,16},{32,24},{40,32},{48,40},{56,48},{64,56},{72,6... | collective-permute-start | bytes 3145736 | tf_op jit(solution)/shard_map/ppermute | solution.py:16
  297.3 149.0 %collective-permute-start.2 = (bf16[128,1,32,128]{3,0,2,1:T(8,128)(2,1)S(1)}, bf16[128,1,32,128]{3,0,2,1:T(8,128)(2,1)S(1)}, u32[]{:S(2)}, u32[]{:S(2)}) collective-permute-start(bf16[128,1,32,128]{3,0,2,1:T(8,128)(2,1)S(1)} %get-tuple-element.6), channel_id=1, source_target_pairs={{0,8},{8,16},{16,24},{24,32},{32,40},{40,48},{48,56},{56,64},{64,7... | collective-permute-start | bytes 3145736 | tf_op jit(solution)/shard_map/ppermute | solution.py:13
  303.1 7.8 %copy-start.10 = (bf16[27,16,128]{2,1,0:T(8,128)(2,1)S(1)}, bf16[27,16,128]{2,1,0:T(8,128)(2,1)}, u32[]{:S(2)}) copy-start(bf16[27,16,128]{2,1,0:T(8,128)(2,1)} %param.4) | copy-start | bytes 331780
  493.9 4.3 copy-start.1
  496.6 3.3 copy-start.3
  506.2 1.2 copy-start.4
  506.2 1.5 copy-start.5
  506.2 1.8 copy-start.6
  506.2 2.1 copy-start.7
  506.2 2.5 copy-start.8
Sparse Core Ops, SparseCore 0:
  52.8 167.6 reduce-scatter.1
  311.0 133.6 all-reduce.3
